TPU v7x, 32 devices: a whole 2x2x4 slice. The times are simulated.
32 devices in a mesh: dp: 16 (over z, x, core), seq: 2 (over y).
Axes of the slice: x: 2, y: 2, z: 4, core: 2. Of those that a mesh axis runs over, the one named last changes fastest.
Arguments:
- images: bfloat16 [32, 592, 1024], P('dp', 'seq'), may hold values from -6 to 6
- cotangent: bfloat16 [32, 592, 1024], P('dp', 'seq'), may hold values from -6 to 6
- w_qkv: float32 [1024, 3072], P('dp', 'seq'), may hold values from -0.1875 to 0.1875
- w_out: float32 [1024, 1024], P('dp', 'seq'), may hold values from -1 to 1
- w_up: float32 [1024, 4096], P('dp', 'seq'), may hold values from -0.1875 to 0.1875
- w_down: float32 [4096, 1024], P('dp', 'seq'), may hold values from -0.09375 to 0.09375
- gains: float32 [2, 1024], P(None, ('dp', 'seq')), may hold values from 0.5 to 1.5
- biases: float32 [10, 1024], P(None, ('dp', 'seq')), may hold values from -3 to 3
- first_qkv: float32 [1024, 3072], P('dp', 'seq'), may hold values from -120 to 120
- first_out: float32 [1024, 1024], P('dp', 'seq'), may hold values from -120 to 120
- first_up: float32 [1024, 4096], P('dp', 'seq'), may hold values from -120 to 120
- first_down: float32 [4096, 1024], P('dp', 'seq'), may hold values from -120 to 120
- first_gains: float32 [2, 1024], P(None, ('dp', 'seq')), may hold values from -120 to 120
- first_biases: float32 [10, 1024], P(None, ('dp', 'seq')), may hold values from -120 to 120
- second_qkv: float32 [1024, 3072], P('dp', 'seq'), may hold values from 100 to 10000
- second_out: float32 [1024, 1024], P('dp', 'seq'), may hold values from 100 to 10000
- second_up: float32 [1024, 4096], P('dp', 'seq'), may hold values from 100 to 10000
- second_down: float32 [4096, 1024], P('dp', 'seq'), may hold values from 100 to 10000
- second_gains: float32 [2, 1024], P(None, ('dp', 'seq')), may hold values from 100 to 10000
- second_biases: float32 [10, 1024], P(None, ('dp', 'seq')), may hold values from 100 to 10000
Outputs:
- out_images: bfloat16 [32, 592, 1024], P('dp', 'seq')
- grad_images: bfloat16 [32, 592, 1024], P('dp', 'seq')
- grad_qkv: float32 [1024, 3072], P('dp', 'seq')
- grad_out: float32 [1024, 1024], P('dp', 'seq')
- grad_up: float32 [1024, 4096], P('dp', 'seq')
- grad_down: float32 [4096, 1024], P('dp', 'seq')
- grad_gains: float32 [2, 1024], P(None, ('dp', 'seq'))
- grad_biases: float32 [10, 1024], P(None, ('dp', 'seq'))
- new_qkv: float32 [1024, 3072], P('dp', 'seq')
- new_out: float32 [1024, 1024], P('dp', 'seq')
- new_up: float32 [1024, 4096], P('dp', 'seq')
- new_down: float32 [4096, 1024], P('dp', 'seq')
- new_gains: float32 [2, 1024], P(None, ('dp', 'seq'))
- new_biases: float32 [10, 1024], P(None, ('dp', 'seq'))
- new_first_qkv: float32 [1024, 3072], P('dp', 'seq')
- new_first_out: float32 [1024, 1024], P('dp', 'seq')
- new_first_up: float32 [1024, 4096], P('dp', 'seq')
- new_first_down: float32 [4096, 1024], P('dp', 'seq')
- new_first_gains: float32 [2, 1024], P(None, ('dp', 'seq'))
- new_first_biases: float32 [10, 1024], P(None, ('dp', 'seq'))
- new_second_qkv: float32 [1024, 3072], P('dp', 'seq')
- new_second_out: float32 [1024, 1024], P('dp', 'seq')
- new_second_up: float32 [1024, 4096], P('dp', 'seq')
- new_second_down: float32 [4096, 1024], P('dp', 'seq')
- new_second_gains: float32 [2, 1024], P(None, ('dp', 'seq'))
- new_second_biases: float32 [10, 1024], P(None, ('dp', 'seq'))
All inputs are finite; a program needn't handle non-finite values.
Results may differ from a plain program's by a relative error of at most 0.028.
Values may be sent and summed in bfloat16 or wider, within the bound.
A program may use at most 256 MiB of HBM per device.

v0:
```python
import jax
import jax.numpy as jnp
from jax import lax
from jax.sharding import PartitionSpec as P

HEAD_DIM = 64
PATCH_TOK = 577
STEP = 5


def normalize(rows):
    center = rows - jnp.mean(rows, axis=-1, keepdims=True)
    inverse = lax.rsqrt(jnp.mean(center * center, axis=-1, keepdims=True) + 1e-06)
    return (center * inverse, inverse)


def norm_back(grad_out, normed, inverse, gain):
    scaled = grad_out * gain
    return inverse * (
        scaled
        - jnp.mean(scaled, axis=-1, keepdims=True)
        - normed * jnp.mean(scaled * normed, axis=-1, keepdims=True)
    )


def gelu_value(pre):
    return pre * 0.5 * (1.0 + lax.erf(pre * 0.7071067811865476))


def gelu_slope(pre):
    return (
        0.5 * (1.0 + lax.erf(pre * 0.7071067811865476))
        + pre * jnp.exp(-0.5 * pre * pre) * 0.3989422804014327
    )


def adamw(param, grad, first, second):
    first_new = 0.9 * first + 0.1 * grad
    second_new = 0.95 * second + 0.05 * grad * grad
    step_size = first_new / (1.0 - 0.9**STEP) / (jnp.sqrt(second_new / (1.0 - 0.95**STEP)) + 1e-08)
    return (param - 0.004 * (step_size + 0.05 * param), first_new, second_new)


def body(
    images,
    cotangent,
    w_qkv,
    w_out,
    w_up,
    w_down,
    gains,
    biases,
    first_qkv,
    first_out,
    first_up,
    first_down,
    first_gains,
    first_biases,
    second_qkv,
    second_out,
    second_up,
    second_down,
    second_gains,
    second_biases,
):
    params = (w_qkv, w_out, w_up, w_down, gains, biases)
    firsts = (first_qkv, first_out, first_up, first_down, first_gains, first_biases)
    seconds = (second_qkv, second_out, second_up, second_down, second_gains, second_biases)
    kernels = tuple((param.astype(jnp.bfloat16) for param in params))
    block_parts = (
        lax.all_gather(kernels[0], "seq", axis=1, tiled=True),
        lax.all_gather(kernels[1], "seq", axis=1, tiled=True),
        lax.all_gather(kernels[2], "seq", axis=1, tiled=True),
        lax.all_gather(kernels[3], "seq", axis=1, tiled=True),
        lax.all_gather(kernels[4], "seq", axis=1, tiled=True),
        lax.all_gather(kernels[5], "seq", axis=1, tiled=True),
    )
    wide_qkv, wide_out, wide_up, wide_down, wide_gains, wide_biases = (
        lax.all_gather(block_parts[0], "dp", axis=0, tiled=True),
        lax.all_gather(block_parts[1], "dp", axis=0, tiled=True),
        lax.all_gather(block_parts[2], "dp", axis=0, tiled=True),
        lax.all_gather(block_parts[3], "dp", axis=0, tiled=True),
        lax.all_gather(block_parts[4], "dp", axis=1, tiled=True),
        lax.all_gather(block_parts[5], "dp", axis=1, tiled=True),
    )
    count, group, width = images.shape
    heads = width // HEAD_DIM
    scale = HEAD_DIM ** (-0.5)
    pad_len = group * lax.axis_size("seq")
    offset = lax.axis_index("seq") * group
    query_live = offset + jnp.arange(group, dtype=jnp.int32) < PATCH_TOK
    key_live = jnp.arange(pad_len, dtype=jnp.int32) < PATCH_TOK
    gain = wide_gains.astype(jnp.float32)
    bias = wide_biases.astype(jnp.float32)
    rows = images.astype(jnp.float32)
    normed_a, inverse_a = normalize(rows)
    hidden_a = (normed_a * gain[0] + bias[0]).astype(jnp.bfloat16)
    mixed = jnp.einsum("icd,de->ice", hidden_a, wide_qkv, preferred_element_type=jnp.float32)
    queries = (mixed[..., :width] + bias[1]).astype(jnp.bfloat16)
    keys = mixed[..., width : 2 * width].astype(jnp.bfloat16)
    values = (mixed[..., 2 * width :] + bias[2]).astype(jnp.bfloat16)
    keys_all, values_all = (
        lax.all_gather(keys, "seq", axis=1, tiled=True),
        lax.all_gather(values, "seq", axis=1, tiled=True),
    )
    query_heads = queries.reshape(count, group, heads, HEAD_DIM)
    key_heads = keys_all.reshape(count, pad_len, heads, HEAD_DIM)
    value_heads = values_all.reshape(count, pad_len, heads, HEAD_DIM)

    def score_block():
        scores = (
            jnp.einsum(
                "ichd,ishd->ihcs", query_heads, key_heads, preferred_element_type=jnp.float32
            )
            * scale
        )
        return jnp.where(key_live[None, None, None, :], scores, -1e30)

    scores = score_block()
    top = jnp.max(scores, axis=-1, keepdims=True)
    lse = top + jnp.log(jnp.sum(jnp.exp(scores - top), axis=-1, keepdims=True))
    probs_b = jnp.exp(scores - lse).astype(jnp.bfloat16)
    context = (
        jnp.einsum("ihcs,ishd->ichd", probs_b, value_heads, preferred_element_type=jnp.float32)
        .reshape(count, group, width)
        .astype(jnp.bfloat16)
    )
    resid = (
        rows
        + jnp.einsum("icd,de->ice", context, wide_out, preferred_element_type=jnp.float32)
        + bias[3]
    )
    normed_b, inverse_b = normalize(resid)
    hidden_b = (normed_b * gain[1] + bias[4]).astype(jnp.bfloat16)
    pre = jnp.einsum("icd,df->icf", hidden_b, wide_up, preferred_element_type=jnp.float32) + bias[
        6:
    ].reshape(-1)
    active = gelu_value(pre).astype(jnp.bfloat16)
    out_images = (
        resid
        + jnp.einsum("icf,fd->icd", active, wide_down, preferred_element_type=jnp.float32)
        + bias[5]
    ).astype(jnp.bfloat16)
    back_qkv, back_out, back_up, back_down, back_gains = (
        wide_qkv,
        wide_out,
        wide_up,
        wide_down,
        wide_gains,
    )
    back_gain = back_gains.astype(jnp.float32)
    grad_y = cotangent.astype(jnp.float32) * query_live[None, :, None].astype(jnp.float32)
    grad_yb = grad_y.astype(jnp.bfloat16)
    g_down = jnp.einsum("icf,icd->fd", active, grad_yb, preferred_element_type=jnp.float32)
    grad_pre = jnp.einsum(
        "icd,fd->icf", grad_yb, back_down, preferred_element_type=jnp.float32
    ) * gelu_slope(pre)
    grad_preb = grad_pre.astype(jnp.bfloat16)
    g_up = jnp.einsum("icd,icf->df", hidden_b, grad_preb, preferred_element_type=jnp.float32)
    grad_hb = jnp.einsum("icf,df->icd", grad_preb, back_up, preferred_element_type=jnp.float32)
    grad_resid = grad_y + norm_back(grad_hb, normed_b, inverse_b, back_gain[1])
    grad_rb = grad_resid.astype(jnp.bfloat16)
    g_outw = jnp.einsum("icd,ice->de", context, grad_rb, preferred_element_type=jnp.float32)
    grad_ctx = (
        jnp.einsum("ice,de->icd", grad_rb, back_out, preferred_element_type=jnp.float32)
        .astype(jnp.bfloat16)
        .reshape(count, group, heads, HEAD_DIM)
    )
    probs = jnp.exp(score_block() - lse)
    grad_probs = jnp.einsum(
        "ichd,ishd->ihcs", grad_ctx, value_heads, preferred_element_type=jnp.float32
    )
    part_v = jnp.einsum(
        "ihcs,ichd->ishd", probs.astype(jnp.bfloat16), grad_ctx, preferred_element_type=jnp.float32
    ).reshape(count, pad_len, width)
    delta = jnp.sum(probs * grad_probs, axis=-1, keepdims=True)
    grad_scores = (probs * (grad_probs - delta) * scale).astype(jnp.bfloat16)
    grad_q = jnp.einsum(
        "ihcs,ishd->ichd", grad_scores, key_heads, preferred_element_type=jnp.float32
    ).reshape(count, group, width)
    part_k = jnp.einsum(
        "ihcs,ichd->ishd", grad_scores, query_heads, preferred_element_type=jnp.float32
    ).reshape(count, pad_len, width)
    grad_k, grad_v = (
        lax.psum_scatter(
            part_k.astype(jnp.bfloat16), "seq", scatter_dimension=1, tiled=True
        ).astype(jnp.float32),
        lax.psum_scatter(
            part_v.astype(jnp.bfloat16), "seq", scatter_dimension=1, tiled=True
        ).astype(jnp.float32),
    )
    grad_mixed = jnp.concatenate([grad_q, grad_k, grad_v], axis=-1).astype(jnp.bfloat16)
    g_qkv = jnp.einsum("icd,ice->de", hidden_a, grad_mixed, preferred_element_type=jnp.float32)
    grad_ha = jnp.einsum("ice,de->icd", grad_mixed, back_qkv, preferred_element_type=jnp.float32)
    grad_images = (grad_resid + norm_back(grad_ha, normed_a, inverse_a, back_gain[0])).astype(
        jnp.bfloat16
    )
    g_gains = jnp.stack(
        [jnp.sum(grad_ha * normed_a, axis=(0, 1)), jnp.sum(grad_hb * normed_b, axis=(0, 1))]
    )
    g_biases = jnp.concatenate(
        [
            jnp.stack(
                [
                    jnp.sum(grad_ha, axis=(0, 1)),
                    jnp.sum(grad_q, axis=(0, 1)),
                    jnp.sum(grad_v, axis=(0, 1)),
                    jnp.sum(grad_resid, axis=(0, 1)),
                    jnp.sum(grad_hb, axis=(0, 1)),
                    jnp.sum(grad_y, axis=(0, 1)),
                ]
            ),
            jnp.sum(grad_pre, axis=(0, 1)).reshape(-1, width),
        ],
        axis=0,
    )
    partial_sums = (
        lax.psum_scatter(g_qkv.astype(jnp.bfloat16), "dp", scatter_dimension=0, tiled=True).astype(
            jnp.float32
        ),
        lax.psum_scatter(g_outw.astype(jnp.bfloat16), "dp", scatter_dimension=0, tiled=True).astype(
            jnp.float32
        ),
        lax.psum_scatter(g_up.astype(jnp.bfloat16), "dp", scatter_dimension=0, tiled=True).astype(
            jnp.float32
        ),
        lax.psum_scatter(g_down.astype(jnp.bfloat16), "dp", scatter_dimension=0, tiled=True).astype(
            jnp.float32
        ),
        lax.psum_scatter(
            g_gains.astype(jnp.bfloat16), "dp", scatter_dimension=1, tiled=True
        ).astype(jnp.float32),
        lax.psum_scatter(
            g_biases.astype(jnp.bfloat16), "dp", scatter_dimension=1, tiled=True
        ).astype(jnp.float32),
    )
    totals = (
        lax.psum_scatter(
            partial_sums[0].astype(jnp.bfloat16), "seq", scatter_dimension=1, tiled=True
        ).astype(jnp.float32),
        lax.psum_scatter(
            partial_sums[1].astype(jnp.bfloat16), "seq", scatter_dimension=1, tiled=True
        ).astype(jnp.float32),
        lax.psum_scatter(
            partial_sums[2].astype(jnp.bfloat16), "seq", scatter_dimension=1, tiled=True
        ).astype(jnp.float32),
        lax.psum_scatter(
            partial_sums[3].astype(jnp.bfloat16), "seq", scatter_dimension=1, tiled=True
        ).astype(jnp.float32),
        lax.psum_scatter(
            partial_sums[4].astype(jnp.bfloat16), "seq", scatter_dimension=1, tiled=True
        ).astype(jnp.float32),
        lax.psum_scatter(
            partial_sums[5].astype(jnp.bfloat16), "seq", scatter_dimension=1, tiled=True
        ).astype(jnp.float32),
    )
    updated = [
        adamw(param, grad, first, second)
        for param, grad, first, second in zip(params, totals, firsts, seconds)
    ]
    news = tuple((entry[0] for entry in updated))
    new_firsts = tuple((entry[1] for entry in updated))
    new_seconds = tuple((entry[2] for entry in updated))
    return (
        out_images,
        grad_images,
        totals[0],
        totals[1],
        totals[2],
        totals[3],
        totals[4],
        totals[5],
        news[0],
        news[1],
        news[2],
        news[3],
        news[4],
        news[5],
        new_firsts[0],
        new_firsts[1],
        new_firsts[2],
        new_firsts[3],
        new_firsts[4],
        new_firsts[5],
        new_seconds[0],
        new_seconds[1],
        new_seconds[2],
        new_seconds[3],
        new_seconds[4],
        new_seconds[5],
    )


def solution(mesh):
    return jax.shard_map(
        body,
        mesh=mesh,
        in_specs=(
            P("dp", "seq", None),
            P("dp", "seq", None),
            P("dp", "seq"),
            P("dp", "seq"),
            P("dp", "seq"),
            P("dp", "seq"),
            P(None, ("dp", "seq")),
            P(None, ("dp", "seq")),
            P("dp", "seq"),
            P("dp", "seq"),
            P("dp", "seq"),
            P("dp", "seq"),
            P(None, ("dp", "seq")),
            P(None, ("dp", "seq")),
            P("dp", "seq"),
            P("dp", "seq"),
            P("dp", "seq"),
            P("dp", "seq"),
            P(None, ("dp", "seq")),
            P(None, ("dp", "seq")),
        ),
        out_specs=(
            P("dp", "seq", None),
            P("dp", "seq", None),
            P("dp", "seq"),
            P("dp", "seq"),
            P("dp", "seq"),
            P("dp", "seq"),
            P(None, ("dp", "seq")),
            P(None, ("dp", "seq")),
            P("dp", "seq"),
            P("dp", "seq"),
            P("dp", "seq"),
            P("dp", "seq"),
            P(None, ("dp", "seq")),
            P(None, ("dp", "seq")),
            P("dp", "seq"),
            P("dp", "seq"),
            P("dp", "seq"),
            P("dp", "seq"),
            P(None, ("dp", "seq")),
            P(None, ("dp", "seq")),
            P("dp", "seq"),
            P("dp", "seq"),
            P("dp", "seq"),
            P("dp", "seq"),
            P(None, ("dp", "seq")),
            P(None, ("dp", "seq")),
        ),
        check_vma=False,
    )
```

profile of v0, /device:TPU:0, one launch (start us, length us, event | category | flops | bytes accessed | tf_op | source)
XLA Modules:
  0.0 1155.2 jit_solution(3185854335412844673)
XLA Ops:
  22.2 22.7 %all-gather.3 = bf16[16,64,10]{1,2,0:T(8,128)(2,1)S(1)} all-gather(bf16[1,64,10]{1,2,0:T(8,128)(2,1)S(1)} %reshape.162), channel_id=1, replica_groups=mesh['dp'=16,'seq'=2] {'dp'}, dimensions={0}, use_global_device_ids=true | all-gather | bytes 21760 | tf_op jit(solution)/shard_map/all_gather | solution.py:84
  50.0 17.9 %all-gather.1 = bf16[16,64,2]{1,2,0:T(2,128)(2,1)S(1)} all-gather(bf16[1,64,2]{1,2,0:T(2,128)(2,1)S(1)} %reshape.158), channel_id=1, replica_groups=mesh['dp'=16,'seq'=2] {'dp'}, dimensions={0}, use_global_device_ids=true | all-gather | bytes 4352 | tf_op jit(solution)/shard_map/all_gather | solution.py:83
  99.1 14.9 %all_gather.52 = bf16[64,4096]{1,0:T(8,128)(2,1)} all-gather(bf16[64,2048]{1,0:T(8,128)(2,1)S(1)} %convert_element_type.171), channel_id=1, replica_groups=mesh['dp'=16,'seq'=2] {'seq'}, dimensions={1}, use_global_device_ids=true | all-gather | bytes 786432 | tf_op jit(solution)/shard_map/all_gather | solution.py:73
  116.5 15.5 %all-gather.13.cloned.1.call-done = bf16[2,592,1024]{2,1,0:T(8,128)(2,1)} async-done(((bf16[2,296,1024]{2,1,0:T(8,128)(2,1)}), bf16[2,592,1024]{2,1,0:T(8,128)(2,1)}) %all-gather.13.cloned.1.call-update) | async-done | bytes 2424848 | tf_op jit(solution)/shard_map/all_gather | solution.py:104
  136.4 33.9 %all-gather.15.cloned.1.call-done = bf16[2,592,1024]{2,1,0:T(8,128)(2,1)} async-done(((bf16[2,296,1024]{2,1,0:T(8,128)(2,1)}), bf16[2,592,1024]{2,1,0:T(8,128)(2,1)}) %all-gather.15.cloned.1.call-update) | async-done | bytes 2424848 | tf_op jit(solution)/shard_map/all_gather | solution.py:103
  174.7 14.2 %fusion.2 = (f32[2,16,296]{2,1,0:T(8,128)S(1)}, f32[2,16,296,592]{3,2,1,0:T(8,128)}) fusion(pred[592]{0:T(1024)(128)(4,1)S(1)} %iota_compare_fusion, bf16[2,296,16,64]{1,3,2,0:T(8,128)(2,1)S(1)} %bitcast.138, bf16[2,592,16,64]{1,3,2,0:T(8,128)(2,1)} %bitcast.130), kind=kOutput, calls=%fused_computation.7 | convolution fusion | flops 734563072 | bytes 26105424 | tf_op jit(solution)/shard_map/ichd,ishd->ihcs/dot_general | solution.py:112
  219.1 69.8 %all-gather.19.cloned.1.call-done = bf16[1024,4096]{1,0:T(8,128)(2,1)} async-done(((bf16[64,4096]{1,0:T(8,128)(2,1)}), bf16[1024,4096]{1,0:T(8,128)(2,1)}) %all-gather.19.cloned.1.call-update) | async-done | bytes 8388624 | tf_op jit(solution)/shard_map/all_gather | solution.py:81
  288.9 12.0 %multiply_convert_fusion.1 = (bf16[2,296,4096]{2,1,0:T(8,128)(2,1)S(1)}, f32[2,296,4096]{2,1,0:T(8,128)}) fusion(f32[4096]{0:T(1024)S(1)} %bitcast.159, bf16[1024,4096]{1,0:T(8,128)(2,1)} %all-gather.19.cloned.1.call-done, f32[2,296,1024]{2,1,0:T(8,128)} %copy-done.3, f32[1024]{0:T(1024)S(1)} %bitcast.166, f32[1024]{0:T(1024)S(1)} %bitcast.155, ...), kind=kOutput, calls=%fused_computation.21 | convolution fusion | flops 4983635968 | bytes 25391744 | tf_op jit(solution)/shard_map/icd,df->icf/dot_general | solution.py:135
  312.4 102.2 %reduce-scatter.39.cloned.1.call-done = bf16[256,1024]{1,0:T(8,128)(2,1)} async-done(((bf16[4096,1024]{1,0:T(8,128)(2,1)}), bf16[256,1024]{1,0:T(8,128)(2,1)}) %reduce-scatter.39.cloned.1.call-update) | async-done | bytes 524304 | tf_op jit(solution)/shard_map/reduce_scatter | solution.py:227
  414.6 16.5 %reduce-scatter.41.cloned.1.call-done = bf16[256,512]{1,0:T(8,128)(2,1)} async-done(((bf16[256,1024]{1,0:T(8,128)(2,1)}), bf16[256,512]{1,0:T(8,128)(2,1)}) %reduce-scatter.41.cloned.1.call-update) | async-done | bytes 262160 | tf_op jit(solution)/shard_map/reduce_scatter | solution.py:247
  442.4 74.4 %all-gather.21.cloned.1.call-done = bf16[4096,1024]{1,0:T(8,128)(2,1)} async-done(((bf16[256,1024]{1,0:T(8,128)(2,1)}), bf16[4096,1024]{1,0:T(8,128)(2,1)}) %all-gather.21.cloned.1.call-update) | async-done | bytes 8388624 | tf_op jit(solution)/shard_map/all_gather | solution.py:82
  516.8 12.6 %fusion.112 = (bf16[4096]{0:T(1024)(128)(2,1)S(1)}, bf16[2,296,4096]{2,1,0:T(8,128)(2,1)S(1)}) fusion(f32[2,296,4096]{2,1,0:T(8,128)} %get-tuple-element.77, f32[4096]{0:T(1024)S(1)} %bitcast.160, bf16[4096,1024]{1,0:T(8,128)(2,1)} %all-gather.21.cloned.1.call-done, bf16[2,296,1024]{2,1,0:T(8,128)(2,1)S(1)} %copy-done.13, f32[296]{0:T(512)} %copy-done.32), kind=kOutput, calls=%fused_computation.148 | convolution fusion | flops 4996968448 | bytes 24175776 | tf_op jit(solution)/shard_map/icd,fd->icf/dot_general | solution.py:155
  546.8 12.0 %convolution_convert_fusion = bf16[2,16,64,592]{3,2,1,0:T(8,128)(2,1)} fusion(bf16[2,296,16,64]{1,3,2,0:T(8,128)(2,1)S(1)} %bitcast.136, f32[2,16,296]{2,1,0:T(8,128)S(1)} %log_add_fusion, f32[2,16,296,592]{3,2,1,0:T(8,128)} %get-tuple-element.73, pred[592]{0:T(1024)(128)(4,1)S(1)} %iota_compare_fusion), kind=kOutput, calls=%fused_computation.83 | convolution fusion | flops 741392384 | bytes 26105424 | tf_op jit(solution)/shard_map/ihcs,ichd->ishd/dot_general | solution.py:173
  569.7 13.8 %fusion.113 = f32[2,16,296,592]{3,2,1,0:T(8,128)} fusion(bf16[2,296,16,64]{1,3,2,0:T(8,128)(2,1)S(1)} %bitcast.137, bf16[2,592,16,64]{1,3,2,0:T(8,128)(2,1)} %bitcast.128), kind=kOutput, calls=%fused_computation.149 | convolution fusion | flops 717750272 | bytes 26066944 | tf_op jit(solution)/shard_map/ichd,ishd->ihcs/dot_general | solution.py:170
  583.5 70.8 %fusion.59 = bf16[2,16,64,592]{3,2,1,0:T(8,128)(2,1)} fusion(bf16[2,296,16,64]{1,3,2,0:T(8,128)(2,1)} %bitcast.139, f32[2,16,296,592]{3,2,1,0:T(8,128)} %fusion.113, f32[2,16,296]{2,1,0:T(8,128)S(1)} %log_add_fusion, f32[2,16,296,592]{3,2,1,0:T(8,128)} %get-tuple-element.73, pred[592]{0:T(1024)(128)(4,1)S(1)} %iota_compare_fusion), kind=kOutput, calls=%fused_computation.82 | convolution fusion | flops 780654400 | bytes 48535120 | tf_op jit(solution)/shard_map/ihcs,ichd->ishd/dot_general | solution.py:181
  671.2 70.3 %bitcast_convert_fusion.4 = (bf16[2,296,16,64]{1,3,2,0:T(8,128)(2,1)S(1)}, f32[2,16,64,296]{3,2,1,0:T(8,128)}) fusion(bf16[2,592,16,64]{1,3,2,0:T(8,128)(2,1)} %bitcast.131, f32[2,16,296,592]{3,2,1,0:T(8,128)} %fusion.113, f32[2,16,296]{2,1,0:T(8,128)S(1)} %log_add_fusion, f32[2,16,296,592]{3,2,1,0:T(8,128)} %get-tuple-element.73, ...), kind=kOutput, calls=%fused_computation.42 | convolution fusion | flops 780048192 | bytes 50959952 | tf_op jit(solution)/shard_map/ihcs,ishd->ichd/dot_general | solution.py:178
  768.6 12.0 %bitcast_convert_fusion.1 = bf16[1024,4096]{1,0:T(8,128)(2,1)} fusion(bf16[2,296,4096]{2,1,0:T(8,128)(2,1)} %copy-done.47, f32[2,296,1024]{2,1,0:T(8,128)} %copy-done.3, f32[1024]{0:T(1024)S(1)} %bitcast.167, f32[1024]{0:T(1024)S(1)} %bitcast.158, f32[2,296]{1,0:T(2,128)S(1)} %add_rsqrt_fusion, f32[2,296]{1,0:T(2,128)S(1)} %broadcast_multiply_fusion.4), kind=kOutput, calls=%fused_computation.9 | convolution fusion | flops 4973281280 | bytes 15676032 | tf_op jit(solution)/shard_map/icd,icf->df/dot_general | solution.py:159
  781.3 42.9 %reduce-scatter.47.cloned.1.call-done = bf16[64,2]{1,0:T(8,128)(2,1)} async-done(((bf16[1024,2]{1,0:T(8,128)(2,1)}), bf16[64,2]{1,0:T(8,128)(2,1)}) %reduce-scatter.47.cloned.1.call-update) | async-done | bytes 272
  833.7 49.4 %reduce-scatter.51.cloned.1.call-done = bf16[64,10]{1,0:T(8,128)(2,1)} async-done(((bf16[1024,10]{1,0:T(8,128)(2,1)}), bf16[64,10]{1,0:T(8,128)(2,1)}) %reduce-scatter.51.cloned.1.call-update) | async-done | bytes 1296
  894.0 95.6 %reduce-scatter.35.cloned.1.call-done = bf16[64,4096]{1,0:T(8,128)(2,1)} async-done(((bf16[1024,4096]{1,0:T(8,128)(2,1)}), bf16[64,4096]{1,0:T(8,128)(2,1)}) %reduce-scatter.35.cloned.1.call-update) | async-done | bytes 524304 | tf_op jit(solution)/shard_map/reduce_scatter | solution.py:224
  989.6 12.0 %reduce-scatter.33.cloned.1.call-done = bf16[64,512]{1,0:T(8,128)(2,1)} async-done(((bf16[64,1024]{1,0:T(8,128)(2,1)}), bf16[64,512]{1,0:T(8,128)(2,1)}) %reduce-scatter.33.cloned.1.call-update) | async-done | bytes 65552 | tf_op jit(solution)/shard_map/reduce_scatter | solution.py:241
  1014.4 88.2 %reduce-scatter.27.cloned.1.call-done = bf16[64,3072]{1,0:T(8,128)(2,1)} async-done(((bf16[1024,3072]{1,0:T(8,128)(2,1)}), bf16[64,3072]{1,0:T(8,128)(2,1)}) %reduce-scatter.27.cloned.1.call-update) | async-done | bytes 393232 | tf_op jit(solution)/shard_map/reduce_scatter | solution.py:218
  1115.1 15.5 %reduce-scatter.37.cloned.1.call-done = bf16[64,2048]{1,0:T(8,128)(2,1)} async-done(((bf16[64,4096]{1,0:T(8,128)(2,1)}), bf16[64,2048]{1,0:T(8,128)(2,1)}) %reduce-scatter.37.cloned.1.call-update) | async-done | bytes 262160 | tf_op jit(solution)/shard_map/reduce_scatter | solution.py:244
  1133.0 12.9 %reduce-scatter.29.cloned.1.call-done = bf16[64,1536]{1,0:T(8,128)(2,1)} async-done(((bf16[64,3072]{1,0:T(8,128)(2,1)}), bf16[64,1536]{1,0:T(8,128)(2,1)}) %reduce-scatter.29.cloned.1.call-update) | async-done | bytes 196624 | tf_op jit(solution)/shard_map/reduce_scatter | solution.py:238
  (231 shorter events, 237.9 us)
Async XLA Ops:
  7.2 73.1 %all-gather.11.cloned.1.call-start = ((), (), s32[]{:S(2)}) async-start(), calls=%async_computation.14 | async-start | bytes 6684672 | tf_op jit(solution)/shard_map/all_gather | solution.py:79
  17.1 114.9 %all-gather.13.cloned.1.call-start = ((), (), s32[]{:S(2)}) async-start(), calls=%async_computation.15 | async-start | bytes 3637248 | tf_op jit(solution)/shard_map/all_gather | solution.py:104
  69.4 219.5 %copy-start.39 = (f32[1,1024]{1,0:T(1,128)}, f32[1,1024]{1,0:T(1,128)S(1)}, u32[]{:S(2)}) copy-start(f32[1,1024]{1,0:T(1,128)S(1)} %get-tuple-element.65) | copy-start | bytes 12292
  90.7 79.6 %all-gather.15.cloned.1.call-start = ((), (), s32[]{:S(2)}) async-start(), calls=%async_computation.16 | async-start | bytes 3637248 | tf_op jit(solution)/shard_map/all_gather | solution.py:103
  93.8 120.0 %all-gather.17.cloned.1.call-start = ((), (), s32[]{:S(2)}) async-start(), calls=%async_computation.17 | async-start | bytes 2228224 | tf_op jit(solution)/shard_map/all_gather | solution.py:80
  99.0 189.9 %all-gather.19.cloned.1.call-start = ((), (), s32[]{:S(2)}) async-start(), calls=%async_computation.18 | async-start | bytes 8912896 | tf_op jit(solution)/shard_map/all_gather | solution.py:81
  114.0 300.5 %reduce-scatter.39.cloned.1.call-start = ((), (), s32[]{:S(2)}) async-start(), calls=%async_computation.26 | async-start | bytes 8912896 | tf_op jit(solution)/shard_map/reduce_scatter | solution.py:227
  114.7 186.3 %copy-start.32 = (f32[296]{0:T(512)}, f32[296]{0:T(512)S(1)}, u32[]{:S(2)}) copy-start(f32[296]{0:T(512)S(1)} %fusion.82) | copy-start | bytes 3556
  312.3 118.8 %reduce-scatter.41.cloned.1.call-start = ((), (), s32[]{:S(2)}) async-start(), calls=%async_computation.27 | async-start | bytes 786432 | tf_op jit(solution)/shard_map/reduce_scatter | solution.py:247
  414.6 102.2 %all-gather.21.cloned.1.call-start = ((), (), s32[]{:S(2)}) async-start(), calls=%async_computation.19 | async-start | bytes 8912896 | tf_op jit(solution)/shard_map/all_gather | solution.py:82
  442.3 303.0 %reduce-scatter.45.cloned.1.call-start = ((), (), s32[]{:S(2)}) async-start(), calls=%async_computation.29 | async-start | bytes 3637248
  569.3 180.8 %reduce-scatter.43.cloned.1.call-start = ((), (), s32[]{:S(2)}) async-start(), calls=%async_computation.28 | async-start | bytes 3637248
  664.8 116.0 %reduce-scatter.31.cloned.1.call-start = ((), (), s32[]{:S(2)}) async-start(), calls=%async_computation.22 | async-start | bytes 2228224 | tf_op jit(solution)/shard_map/reduce_scatter | solution.py:221
  671.0 153.2 %reduce-scatter.47.cloned.1.call-start = ((), (), s32[]{:S(2)}) async-start(), calls=%async_computation.30 | async-start | bytes 278528
  766.4 116.7 %reduce-scatter.51.cloned.1.call-start = ((), (), s32[]{:S(2)}) async-start(), calls=%async_computation.32 | async-start | bytes 278528
  768.6 221.0 %reduce-scatter.35.cloned.1.call-start = ((), (), s32[]{:S(2)}) async-start(), calls=%async_computation.24 | async-start | bytes 8912896 | tf_op jit(solution)/shard_map/reduce_scatter | solution.py:224
  780.7 221.0 %reduce-scatter.33.cloned.1.call-start = ((), (), s32[]{:S(2)}) async-start(), calls=%async_computation.23 | async-start | bytes 196608 | tf_op jit(solution)/shard_map/reduce_scatter | solution.py:241
  781.2 232.4 %reduce-scatter.49.cloned.1.call-start = ((), (), s32[]{:S(2)}) async-start(), calls=%async_computation.31 | async-start | bytes 24576
  824.3 278.3 %reduce-scatter.27.cloned.1.call-start = ((), (), s32[]{:S(2)}) async-start(), calls=%async_computation.20 | async-start | bytes 6684672 | tf_op jit(solution)/shard_map/reduce_scatter | solution.py:218
  833.6 280.1 %reduce-scatter.53.cloned.1.call-start = ((), (), s32[]{:S(2)}) async-start(), calls=%async_computation.33 | async-start | bytes 24576
  883.1 247.5 %reduce-scatter.37.cloned.1.call-start = ((), (), s32[]{:S(2)}) async-start(), calls=%async_computation.25 | async-start | bytes 786432 | tf_op jit(solution)/shard_map/reduce_scatter | solution.py:244
  989.6 156.4 %reduce-scatter.29.cloned.1.call-start = ((), (), s32[]{:S(2)}) async-start(), calls=%async_computation.21 | async-start | bytes 589824 | tf_op jit(solution)/shard_map/reduce_scatter | solution.py:238
  1007.8 138.1 %copy-start.21 = (f32[64,1536]{1,0:T(8,128)S(1)}, f32[64,1536]{1,0:T(8,128)}, u32[]{:S(2)}) copy-start(f32[64,1536]{1,0:T(8,128)} %param.28) | copy-start | bytes 1179652
  1007.8 138.1 %copy-start.22 = (f32[64,1536]{1,0:T(8,128)S(1)}, f32[64,1536]{1,0:T(8,128)}, u32[]{:S(2)}) copy-start(f32[64,1536]{1,0:T(8,128)} %param.34) | copy-start | bytes 1179652
  (45 other events, 2205.6 us)
Sparse Core Ops, SparseCore 0:
  17.2 63.0 all-gather.10
  90.9 41.0 all-gather.12
  133.5 36.7 all-gather.14
  172.4 41.4 all-gather.16
  215.8 73.0 all-gather.18
  312.4 102.0 reduce-scatter.38
  416.8 14.2 reduce-scatter.40
  442.4 74.2 all-gather.20
  569.4 34.1 reduce-scatter.44
  664.9 34.8 reduce-scatter.42
  703.5 61.9 reduce-scatter.30
  769.5 54.7 reduce-scatter.46
  828.3 54.7 reduce-scatter.50
  887.0 102.4 reduce-scatter.34
  991.6 9.9 reduce-scatter.32
  1003.7 9.9 reduce-scatter.48
  1017.4 85.1 reduce-scatter.26
  1104.6 9.0 reduce-scatter.52
  1116.0 14.6 reduce-scatter.36
  1132.7 13.1 reduce-scatter.28
where the time goes:
time: 1160 us
  waiting for transfers between devices  662 us (57%)
  matrix products  294 us (25%)
  blocking collectives  86.4 us (7%)
  local copies, waits for them, and re-layouts  61.1 us (5%)
  other arithmetic  34.6 us (3%)
  between operations  15.3 us (1%)
    unnamed x26, waiting for transfers between devices  110 us
    reduce_scatter x1, waiting for transfers between devices, body(): lax.psum_scatter(g_down.astype(jnp.bfloat16), 'dp', scatter_dimension=0,...  102 us
    reduce_scatter x1, waiting for transfers between devices, body(): lax.psum_scatter(g_up.astype(jnp.bfloat16), 'dp', scatter_dimension=0, ti...  95.6 us
    reduce_scatter x1, waiting for transfers between devices, body(): lax.psum_scatter(g_qkv.astype(jnp.bfloat16), 'dp', scatter_dimension=0, t...  88.2 us
    all_gather x1, waiting for transfers between devices, body(): lax.all_gather(block_parts[3], 'dp', axis=0, tiled=True)  74.4 us
    dot_general x1, matrix products, body(): jnp.einsum('ihcs,ichd->ishd', grad_scores, query_heads, preferred_element...  70.8 us
    dot_general x1, matrix products, body(): jnp.einsum('ihcs,ishd->ichd', grad_scores, key_heads, preferred_element_t...  70.3 us
    all_gather x1, waiting for transfers between devices, body(): lax.all_gather(block_parts[2], 'dp', axis=0, tiled=True)  69.8 us
  transfers between devices with their start and end apart: 20, of which 17 were waited for; matrix products, arithmetic and copies ran while one was open for 26% of the time, Pallas kernels for 0%

commit v1 on v0

v1 whole, which is shorter than its diff:
```python
import jax
import jax.numpy as jnp
from jax import lax
from jax.experimental import pallas as pl
from jax.experimental.pallas import tpu as pltpu
from jax.sharding import PartitionSpec as P

HEAD_DIM = 64
PATCH_TOK = 577
STEP = 5


def normalize(rows):
    center = rows - jnp.mean(rows, axis=-1, keepdims=True)
    inverse = lax.rsqrt(jnp.mean(center * center, axis=-1, keepdims=True) + 1e-06)
    return (center * inverse, inverse)


def norm_back(grad_out, normed, inverse, gain):
    scaled = grad_out * gain
    return inverse * (
        scaled
        - jnp.mean(scaled, axis=-1, keepdims=True)
        - normed * jnp.mean(scaled * normed, axis=-1, keepdims=True)
    )


def gelu_value(pre):
    return pre * 0.5 * (1.0 + lax.erf(pre * 0.7071067811865476))


def gelu_slope(pre):
    return (
        0.5 * (1.0 + lax.erf(pre * 0.7071067811865476))
        + pre * jnp.exp(-0.5 * pre * pre) * 0.3989422804014327
    )


def adamw(param, grad, first, second):
    first_new = 0.9 * first + 0.1 * grad
    second_new = 0.95 * second + 0.05 * grad * grad
    step_size = first_new / (1.0 - 0.9**STEP) / (jnp.sqrt(second_new / (1.0 - 0.95**STEP)) + 1e-08)
    return (param - 0.004 * (step_size + 0.05 * param), first_new, second_new)


LANES = 128
NT = (((1,), (1,)), ((), ()))
NN = (((1,), (0,)), ((), ()))
TN = (((0,), (0,)), ((), ()))


def dot(a, b, dims):
    return lax.dot_general(a, b, dims, preferred_element_type=jnp.float32)


def head_masks(rows, dtype):
    lane = lax.broadcasted_iota(jnp.int32, (rows, LANES), 1)
    return [
        ((lane >= h * HEAD_DIM) & (lane < (h + 1) * HEAD_DIM)) for h in range(LANES // HEAD_DIM)
    ]


def attend_kernel(q_ref, k_ref, v_ref, live_ref, ctx_ref):
    q, k, v = q_ref[0], k_ref[0], v_ref[0]
    live = live_ref[...] > 0.5
    total = jnp.zeros(q.shape, jnp.float32)
    zero = jnp.zeros_like(q)
    for mask in head_masks(q.shape[0], q.dtype):
        scores = dot(jnp.where(mask, q, zero), k, NT) * (HEAD_DIM**-0.5)
        scores = jnp.where(live, scores, -1e30)
        top = jnp.max(scores, axis=-1, keepdims=True)
        weights = jnp.exp(scores - top)
        denom = jnp.sum(weights, axis=-1, keepdims=True)
        probs = (weights * (1.0 / denom)).astype(jnp.bfloat16)
        total = jnp.where(mask, dot(probs, v, NN), total)
    ctx_ref[0] = total.astype(jnp.bfloat16)


def attend_back_kernel(q_ref, k_ref, v_ref, g_ref, live_ref, dq_ref, dk_ref, dv_ref):
    q, k, v, g = q_ref[0], k_ref[0], v_ref[0], g_ref[0]
    live = live_ref[...] > 0.5
    zero_q = jnp.zeros_like(q)
    zero_k = jnp.zeros_like(k)
    dq = jnp.zeros(q.shape, jnp.float32)
    dk = jnp.zeros(k.shape, jnp.float32)
    dv = jnp.zeros(k.shape, jnp.float32)
    masks_q = head_masks(q.shape[0], q.dtype)
    masks_k = head_masks(k.shape[0], k.dtype)
    for mask, mask_k in zip(masks_q, masks_k):
        q_h = jnp.where(mask, q, zero_q)
        g_h = jnp.where(mask, g, zero_q)
        k_h = jnp.where(mask_k, k, zero_k)
        scores = dot(k, q_h, NT) * (HEAD_DIM**-0.5)
        scores = jnp.where(live, scores, -1e30)
        top = jnp.max(scores, axis=0, keepdims=True)
        weights = jnp.exp(scores - top)
        denom = jnp.sum(weights, axis=0, keepdims=True)
        probs = weights * (1.0 / denom)
        grad_probs = dot(v, g_h, NT)
        delta = jnp.sum(probs * grad_probs, axis=0, keepdims=True)
        grad_scores = (probs * (grad_probs - delta) * (HEAD_DIM**-0.5)).astype(jnp.bfloat16)
        dv = dv + dot(probs.astype(jnp.bfloat16), g_h, NN)
        dk = dk + dot(grad_scores, q_h, NN)
        dq = dq + dot(grad_scores, k_h, TN)
    dq_ref[0] = dq
    dk_ref[0] = dk.astype(dk_ref.dtype)
    dv_ref[0] = dv.astype(dv_ref.dtype)


def attend(queries, keys, values, live):
    count, rows, width = queries.shape
    length = keys.shape[1]
    q_spec = pl.BlockSpec((1, rows, LANES), lambda i, h: (i, 0, h))
    k_spec = pl.BlockSpec((1, length, LANES), lambda i, h: (i, 0, h))
    pairs = count * rows * length * width
    return pl.pallas_call(
        attend_kernel,
        grid=(count, width // LANES),
        in_specs=[q_spec, k_spec, k_spec, pl.BlockSpec((1, length), lambda i, h: (0, 0))],
        out_specs=q_spec,
        out_shape=jax.ShapeDtypeStruct(queries.shape, jnp.bfloat16),
        cost_estimate=pl.CostEstimate(
            flops=8 * pairs, bytes_accessed=8 * queries.size, transcendentals=pairs // HEAD_DIM
        ),
        compiler_params=pltpu.CompilerParams(vmem_limit_bytes=48 * 1024 * 1024),
    )(queries, keys, values, live.reshape(1, length))


def attend_back(queries, keys, values, grad_ctx, live, back_dtype):
    count, rows, width = queries.shape
    length = keys.shape[1]
    q_spec = pl.BlockSpec((1, rows, LANES), lambda i, h: (i, 0, h))
    k_spec = pl.BlockSpec((1, length, LANES), lambda i, h: (i, 0, h))
    pairs = count * rows * length * width
    return pl.pallas_call(
        attend_back_kernel,
        grid=(count, width // LANES),
        in_specs=[q_spec, k_spec, k_spec, q_spec, pl.BlockSpec((length, 1), lambda i, h: (0, 0))],
        out_specs=[q_spec, k_spec, k_spec],
        out_shape=[
            jax.ShapeDtypeStruct(queries.shape, jnp.float32),
            jax.ShapeDtypeStruct(keys.shape, back_dtype),
            jax.ShapeDtypeStruct(keys.shape, back_dtype),
        ],
        cost_estimate=pl.CostEstimate(
            flops=20 * pairs, bytes_accessed=20 * queries.size, transcendentals=pairs // HEAD_DIM
        ),
        compiler_params=pltpu.CompilerParams(vmem_limit_bytes=56 * 1024 * 1024),
    )(queries, keys, values, grad_ctx, live.reshape(length, 1))


def shift_by(step, ways):
    return [(i, (i + step) % ways) for i in range(ways)]


def spread(tokens):
    ways = lax.axis_size("seq")
    me = lax.axis_index("seq")
    each = tokens.shape[0] // ways
    parts = [lax.dynamic_slice_in_dim(tokens, me * each, each, 0)]
    for step in range(1, ways):
        target = lax.rem(me + step, ways)
        piece = lax.dynamic_slice_in_dim(tokens, target * each, each, 0)
        parts.append(lax.ppermute(piece, "seq", shift_by(step, ways)))
    return jnp.concatenate(parts, axis=1)


def unspread(tokens):
    ways = lax.axis_size("seq")
    me = lax.axis_index("seq")
    each, length, width = tokens.shape
    group = length // ways
    result = jnp.zeros((each * ways, group, width), tokens.dtype)
    for step in range(ways):
        piece = tokens[:, step * group : (step + 1) * group]
        if step:
            piece = lax.ppermute(piece, "seq", shift_by(-step, ways))
        source = lax.rem(me + step, ways)
        result = lax.dynamic_update_slice_in_dim(result, piece, source * each, 0)
    return result


def sum_over_seq(terms, axis):
    ways = lax.axis_size("seq")
    me = lax.axis_index("seq")
    size = terms.shape[axis] // ways
    total = lax.dynamic_slice_in_dim(terms, me * size, size, axis).astype(jnp.float32)
    for step in range(1, ways):
        target = lax.rem(me + step, ways)
        piece = lax.dynamic_slice_in_dim(terms, target * size, size, axis)
        total = total + lax.ppermute(piece, "seq", shift_by(step, ways)).astype(jnp.float32)
    return total


def body(
    images,
    cotangent,
    w_qkv,
    w_out,
    w_up,
    w_down,
    gains,
    biases,
    first_qkv,
    first_out,
    first_up,
    first_down,
    first_gains,
    first_biases,
    second_qkv,
    second_out,
    second_up,
    second_down,
    second_gains,
    second_biases,
):
    params = (w_qkv, w_out, w_up, w_down, gains, biases)
    firsts = (first_qkv, first_out, first_up, first_down, first_gains, first_biases)
    seconds = (second_qkv, second_out, second_up, second_down, second_gains, second_biases)
    count, group, width = images.shape
    ways = lax.axis_size("seq")
    blocks = lax.axis_size("dp")
    me = lax.axis_index("seq")
    pad_len = group * ways
    by_image = count % ways == 0
    rows_dp = w_qkv.shape[0]
    cols = w_out.shape[1]
    fold = w_up.shape[1] // cols
    own = gains.shape[1]
    small = jnp.concatenate([gains, biases], axis=0).astype(jnp.bfloat16).T
    lanes = -(-small.shape[1] // LANES) * LANES
    small = jnp.pad(small, ((0, rows_dp - own), (0, lanes - small.shape[1])))
    part_a = jnp.concatenate([w_qkv.astype(jnp.bfloat16), small], axis=1)
    wide_a = lax.all_gather(part_a, ("seq", "dp"), axis=0, tiled=True)
    part_b = jnp.concatenate(
        [
            w_out.astype(jnp.bfloat16),
            w_up.astype(jnp.bfloat16)
            .reshape(rows_dp, fold, cols)
            .transpose(1, 0, 2)
            .reshape(fold * rows_dp, cols),
            w_down.astype(jnp.bfloat16),
        ],
        axis=0,
    )
    part_b, wide_a = lax.optimization_barrier((part_b, wide_a))
    wide_b = lax.all_gather(part_b, ("seq", "dp"), axis=0, tiled=True)
    wide_a = wide_a.reshape(ways, width, part_a.shape[1])
    wide_qkv = jnp.concatenate([wide_a[k, :, : w_qkv.shape[1]] for k in range(ways)], axis=1)
    wide_small = (
        wide_a.reshape(ways, blocks, rows_dp, part_a.shape[1])[
            :, :, :own, w_qkv.shape[1] : w_qkv.shape[1] + 12
        ]
        .astype(jnp.float32)
        .transpose(3, 1, 0, 2)
        .reshape(12, width)
    )
    gain, bias = wide_small[:2], wide_small[2:]
    back_gain = gain
    wide_b = wide_b.reshape(ways, blocks, part_b.shape[0], cols)
    wide_out = wide_b[:, :, :rows_dp].transpose(1, 2, 0, 3).reshape(width, width)
    wide_up = (
        wide_b[:, :, rows_dp : (1 + fold) * rows_dp]
        .reshape(ways, blocks, fold, rows_dp, cols)
        .transpose(1, 3, 0, 2, 4)
        .reshape(width, fold * width)
    )
    wide_down = (
        wide_b[:, :, (1 + fold) * rows_dp :].transpose(1, 2, 0, 3).reshape(fold * width, width)
    )
    back_qkv, back_out, back_up, back_down = wide_qkv, wide_out, wide_up, wide_down
    spot = jnp.arange(group, dtype=jnp.int32)
    if by_image:
        images, cotangent = spread(images), spread(cotangent)
        token_live = jnp.concatenate(
            [lax.rem(me - k + ways, ways) * group + spot for k in range(ways)]
        ) < PATCH_TOK
        key_live = token_live
    else:
        token_live = me * group + spot < PATCH_TOK
        key_live = jnp.arange(pad_len, dtype=jnp.int32) < PATCH_TOK
    query_live = token_live
    key_live = key_live.astype(jnp.float32)
    rows = images.astype(jnp.float32)
    normed_a, inverse_a = normalize(rows)
    hidden_a = (normed_a * gain[0] + bias[0]).astype(jnp.bfloat16)
    mixed = jnp.einsum("icd,de->ice", hidden_a, wide_qkv, preferred_element_type=jnp.float32)
    queries = (mixed[..., :width] + bias[1]).astype(jnp.bfloat16)
    keys = mixed[..., width : 2 * width].astype(jnp.bfloat16)
    values = (mixed[..., 2 * width :] + bias[2]).astype(jnp.bfloat16)
    if by_image:
        keys_all, values_all = keys, values
    else:
        keys_all, values_all = (
            lax.all_gather(keys, "seq", axis=1, tiled=True),
            lax.all_gather(values, "seq", axis=1, tiled=True),
        )
    context = attend(queries, keys_all, values_all, key_live)
    resid = (
        rows
        + jnp.einsum("icd,de->ice", context, wide_out, preferred_element_type=jnp.float32)
        + bias[3]
    )
    normed_b, inverse_b = normalize(resid)
    hidden_b = (normed_b * gain[1] + bias[4]).astype(jnp.bfloat16)
    pre = jnp.einsum("icd,df->icf", hidden_b, wide_up, preferred_element_type=jnp.float32) + bias[
        6:
    ].reshape(-1)
    active = gelu_value(pre).astype(jnp.bfloat16)
    out_images = (
        resid
        + jnp.einsum("icf,fd->icd", active, wide_down, preferred_element_type=jnp.float32)
        + bias[5]
    ).astype(jnp.bfloat16)
    grad_y = cotangent.astype(jnp.float32) * query_live[None, :, None].astype(jnp.float32)
    grad_yb = grad_y.astype(jnp.bfloat16)
    g_down = jnp.einsum("icf,icd->fd", active, grad_yb, preferred_element_type=jnp.float32)
    grad_pre = jnp.einsum(
        "icd,fd->icf", grad_yb, back_down, preferred_element_type=jnp.float32
    ) * gelu_slope(pre)
    grad_preb = grad_pre.astype(jnp.bfloat16)
    g_up = jnp.einsum("icd,icf->df", hidden_b, grad_preb, preferred_element_type=jnp.float32)
    grad_hb = jnp.einsum("icf,df->icd", grad_preb, back_up, preferred_element_type=jnp.float32)
    grad_resid = grad_y + norm_back(grad_hb, normed_b, inverse_b, back_gain[1])
    grad_rb = grad_resid.astype(jnp.bfloat16)
    g_outw = jnp.einsum("icd,ice->de", context, grad_rb, preferred_element_type=jnp.float32)
    grad_ctx = jnp.einsum(
        "ice,de->icd", grad_rb, back_out, preferred_element_type=jnp.float32
    ).astype(jnp.bfloat16)
    grad_q, grad_k, grad_v = attend_back(
        queries,
        keys_all,
        values_all,
        grad_ctx,
        key_live,
        jnp.float32 if by_image else jnp.bfloat16,
    )
    if not by_image:
        grad_k, grad_v = (
            lax.psum_scatter(grad_k, "seq", scatter_dimension=1, tiled=True).astype(jnp.float32),
            lax.psum_scatter(grad_v, "seq", scatter_dimension=1, tiled=True).astype(jnp.float32),
        )
    grad_mixed = jnp.concatenate([grad_q, grad_k, grad_v], axis=-1).astype(jnp.bfloat16)
    g_qkv = jnp.einsum("icd,ice->de", hidden_a, grad_mixed, preferred_element_type=jnp.float32)
    grad_ha = jnp.einsum("ice,de->icd", grad_mixed, back_qkv, preferred_element_type=jnp.float32)
    grad_images = (grad_resid + norm_back(grad_ha, normed_a, inverse_a, back_gain[0])).astype(
        jnp.bfloat16
    )
    g_gains = jnp.stack(
        [jnp.sum(grad_ha * normed_a, axis=(0, 1)), jnp.sum(grad_hb * normed_b, axis=(0, 1))]
    )
    g_biases = jnp.concatenate(
        [
            jnp.stack(
                [
                    jnp.sum(grad_ha, axis=(0, 1)),
                    jnp.sum(grad_q, axis=(0, 1)),
                    jnp.sum(grad_v, axis=(0, 1)),
                    jnp.sum(grad_resid, axis=(0, 1)),
                    jnp.sum(grad_hb, axis=(0, 1)),
                    jnp.sum(grad_y, axis=(0, 1)),
                ]
            ),
            jnp.sum(grad_pre, axis=(0, 1)).reshape(-1, width),
        ],
        axis=0,
    )
    if by_image:
        out_images, grad_images = unspread(out_images), unspread(grad_images)
    send_a = jnp.concatenate(
        [
            g_outw.astype(jnp.bfloat16).reshape(blocks, rows_dp, width),
            g_up.astype(jnp.bfloat16)
            .reshape(blocks, rows_dp, ways, fold, cols)
            .transpose(0, 3, 1, 2, 4)
            .reshape(blocks, fold * rows_dp, width),
            g_down.astype(jnp.bfloat16).reshape(blocks, fold * rows_dp, width),
        ],
        axis=1,
    ).reshape(-1, width)
    part = lax.psum_scatter(send_a, "dp", scatter_dimension=0, tiled=True)
    total_a = sum_over_seq(part, 1)
    g_small = jnp.concatenate([g_gains, g_biases], axis=0).astype(jnp.bfloat16).T
    g_small = jnp.pad(g_small, ((0, 0), (0, lanes - g_small.shape[1])))
    send_b = jnp.concatenate([g_qkv.astype(jnp.bfloat16), g_small], axis=1)
    part, _ = lax.optimization_barrier((send_b, part))
    part = lax.psum_scatter(part, "dp", scatter_dimension=0, tiled=True)
    total_qkv = sum_over_seq(part[:, : g_qkv.shape[1]], 1)
    total_small = sum_over_seq(part[:, g_qkv.shape[1] :], 0)[:, :12].T
    totals = (
        total_qkv,
        total_a[:rows_dp],
        total_a[rows_dp : (1 + fold) * rows_dp]
        .reshape(fold, rows_dp, cols)
        .transpose(1, 0, 2)
        .reshape(rows_dp, fold * cols),
        total_a[(1 + fold) * rows_dp :],
        total_small[:2],
        total_small[2:],
    )
    updated = [
        adamw(param, grad, first, second)
        for param, grad, first, second in zip(params, totals, firsts, seconds)
    ]
    news = tuple((entry[0] for entry in updated))
    new_firsts = tuple((entry[1] for entry in updated))
    new_seconds = tuple((entry[2] for entry in updated))
    return (
        out_images,
        grad_images,
        totals[0],
        totals[1],
        totals[2],
        totals[3],
        totals[4],
        totals[5],
        news[0],
        news[1],
        news[2],
        news[3],
        news[4],
        news[5],
        new_firsts[0],
        new_firsts[1],
        new_firsts[2],
        new_firsts[3],
        new_firsts[4],
        new_firsts[5],
        new_seconds[0],
        new_seconds[1],
        new_seconds[2],
        new_seconds[3],
        new_seconds[4],
        new_seconds[5],
    )


def solution(mesh):
    return jax.shard_map(
        body,
        mesh=mesh,
        in_specs=(
            P("dp", "seq", None),
            P("dp", "seq", None),
            P("dp", "seq"),
            P("dp", "seq"),
            P("dp", "seq"),
            P("dp", "seq"),
            P(None, ("dp", "seq")),
            P(None, ("dp", "seq")),
            P("dp", "seq"),
            P("dp", "seq"),
            P("dp", "seq"),
            P("dp", "seq"),
            P(None, ("dp", "seq")),
            P(None, ("dp", "seq")),
            P("dp", "seq"),
            P("dp", "seq"),
            P("dp", "seq"),
            P("dp", "seq"),
            P(None, ("dp", "seq")),
            P(None, ("dp", "seq")),
        ),
        out_specs=(
            P("dp", "seq", None),
            P("dp", "seq", None),
            P("dp", "seq"),
            P("dp", "seq"),
            P("dp", "seq"),
            P("dp", "seq"),
            P(None, ("dp", "seq")),
            P(None, ("dp", "seq")),
            P("dp", "seq"),
            P("dp", "seq"),
            P("dp", "seq"),
            P("dp", "seq"),
            P(None, ("dp", "seq")),
            P(None, ("dp", "seq")),
            P("dp", "seq"),
            P("dp", "seq"),
            P("dp", "seq"),
            P("dp", "seq"),
            P(None, ("dp", "seq")),
            P(None, ("dp", "seq")),
            P("dp", "seq"),
            P("dp", "seq"),
            P("dp", "seq"),
            P("dp", "seq"),
            P(None, ("dp", "seq")),
            P(None, ("dp", "seq")),
        ),
        check_vma=False,
    )
```

time: 1160 us -> 717 us (0.62)
  waiting for transfers between devices: 662 us -> 351 us
  matrix products: 294 us -> 89.5 us
  blocking collectives: 86.4 us -> 0 us
  local copies, waits for them, and re-layouts: 61.1 us -> 141 us
  Pallas kernels: 0 us -> 50.7 us
  other arithmetic: 34.6 us -> 55.1 us
    reduce_scatter x8 -> x1, waiting for transfers between devices: 343 us -> 127 us  [body(): part = lax.psum_scatter(send_a, 'dp', scatter_dimension=0, tiled=True)]
    dot_general x6 -> x0, matrix products: 192 us -> none  [the longest x1 70.8 us: body(): jnp.einsum('ihcs,ichd->ishd', grad_scores, query_heads, preferred_element...]
    all_gather x8 -> x0, blocking collectives: 86.4 us -> none  [the longest x1 22.7 us: body(): lax.all_gather(block_parts[5], 'dp', axis=1, tiled=True)]
    unnamed x26 -> x5, waiting for transfers between devices: 110 us -> 31.2 us
    all_gather x6 -> x2, waiting for transfers between devices: 209 us -> 141 us  [the longest x1 71.5 us: body(): wide_a = lax.all_gather(part_a, ('seq', 'dp'), axis=0, tiled=True)]
    reshape x1 -> x6, local copies, waits for them, and re-layouts: 1.51 us -> 56.3 us  [the longest x3 41.8 us: body(): send_a = jnp.concatenate([g_outw.astype(jnp.bfloat16).reshape(blocks, row...]
    ppermute x0 -> x7, waiting for transfers between devices: none -> 51.6 us  [the longest x2 17.7 us: unspread(): piece = lax.ppermute(piece, 'seq', shift_by(-step, ways))]
    pallas_call x0 -> x2, Pallas kernels: none -> 50.7 us  [the longest x1 33.4 us: attend_back(): pl.pallas_call(attend_back_kernel, grid=(count, width // LANES), in_specs...]
  transfers between devices with their start and end apart: 20 -> 11, of which waited for: 17 -> 10; matrix products, arithmetic and copies ran while one was open for 26% -> 23% of each run, Pallas kernels for 0% -> 7%
where the time goes in v1:
time: 717 us; the launch traced here: 710 us
  waiting for transfers between devices  351 us (49%)
  local copies, waits for them, and re-layouts  141 us (20%)
  matrix products  89.5 us (12%)
  other arithmetic  55.1 us (8%)
  Pallas kernels  50.7 us (7%)
  between operations  15.1 us (2%)
  starting transfers between devices  7.78 us (1%)
    reduce_scatter x1, waiting for transfers between devices, body(): part = lax.psum_scatter(send_a, 'dp', scatter_dimension=0, tiled=True)  127 us
    all_gather x1, waiting for transfers between devices, body(): wide_a = lax.all_gather(part_a, ('seq', 'dp'), axis=0, tiled=True)  71.5 us
    all_gather x1, waiting for transfers between devices, body(): wide_b = lax.all_gather(part_b, ('seq', 'dp'), axis=0, tiled=True)  69.8 us
    reshape x3, local copies, waits for them, and re-layouts, body(): send_a = jnp.concatenate([g_outw.astype(jnp.bfloat16).reshape(blocks, row...  41.8 us
    pallas_call x1, Pallas kernels, attend_back(): pl.pallas_call(attend_back_kernel, grid=(count, width // LANES), in_specs...  33.4 us
    unnamed x141, local copies, waits for them, and re-layouts  32.9 us
    unnamed x5, waiting for transfers between devices  31.2 us
    transpose x2, local copies, waits for them, and re-layouts, body(): wide_b[:, :, (1 + fold) * rows_dp:].transpose(1, 2, 0, 3)  24.3 us
  transfers between devices with their start and end apart: 11, of which 10 were waited for; matrix products, arithmetic and copies ran while one was open for 23% of the time, Pallas kernels for 7%

profile of v1, /device:TPU:0, one launch (start us, length us, event | category | flops | bytes accessed | tf_op | source)
XLA Modules:
  0.0 709.9 jit_solution(6612714012748631889)
XLA Ops:
  13.7 71.5 %all-gather.3.cloned.1.call-done = bf16[2048,1664]{1,0:T(8,128)(2,1)} async-done(((bf16[64,1664]{1,0:T(8,128)(2,1)}), bf16[2048,1664]{1,0:T(8,128)(2,1)}) %all-gather.3.cloned.1.call-update) | async-done | bytes 6815760 | tf_op jit(solution)/shard_map/all_gather | solution.py:234
  89.5 17.6 %collective-permute-done = bf16[1,296,1024]{2,1,0:T(8,128)(2,1)S(1)} collective-permute-done((bf16[1,296,1024]{2,1,0:T(8,128)(2,1)}, bf16[1,296,1024]{2,1,0:T(8,128)(2,1)S(1)}, u32[]{:S(2)}, u32[]{:S(2)}) %collective-permute-start) | collective-permute-done | bytes 606240 | tf_op jit(solution)/shard_map/ppermute | solution.py:164
  124.5 17.3 %shard_map.395 = bf16[1,592,1024]{2,1,0:T(8,128)(2,1)S(1)} custom-call(bf16[1,592,1024]{2,1,0:T(8,128)(2,1)S(1)} %get-tuple-element.229.q_ref, bf16[1,592,1024]{2,1,0:T(8,128)(2,1)S(1)} %slice.191.k_ref, bf16[1,592,1024]{2,1,0:T(8,128)(2,1)S(1)} %get-tuple-element.228.v_ref, f32[1,592]{1,0:T(1,128)S(1)} %compare_convert_fusion.1.live_ref), custom_call_target="tpu_custom_call" | custom-call | flops 2871001088 | bytes 4849664 | tf_op jit(solution)/shard_map/pallas_call | solution.py:116
  143.8 69.8 %all-gather.5.cloned.1.call-done = bf16[18432,512]{1,0:T(8,128)(2,1)} async-done(((bf16[576,512]{1,0:T(8,128)(2,1)}), bf16[18432,512]{1,0:T(8,128)(2,1)}) %all-gather.5.cloned.1.call-update) | async-done | bytes 18874384 | tf_op jit(solution)/shard_map/all_gather | solution.py:247
  215.5 9.3 %slice_bitcast_fusion = (bf16[16,256,2,512]{3,1,0,2:T(8,128)(2,1)}, bf16[2,16,256,512]{3,2,1,0:T(8,128)(2,1)S(1)}) fusion(bf16[2,16,576,512]{3,2,1,0:T(8,128)(2,1)} %bitcast.97), kind=kLoop, calls=%fused_computation.11 | loop fusion | bytes 33554432 | tf_op jit(solution)/shard_map/transpose | solution.py:269
  236.4 14.5 %reshape.703 = bf16[1024,4096]{1,0:T(8,128)(2,1)} reshape(bf16[16,64,2,4,512]{4,3,2,1,0:T(4,128)(2,1)} %copy.207) | data formatting | bytes 16777216 | tf_op jit(solution)/shard_map/reshape | solution.py:266
  255.0 11.0 %multiply_convert_fusion = (bf16[592,4096]{1,0:T(8,128)(2,1)}, f32[592,4096]{1,0:T(8,128)}) fusion(f32[4096]{0:T(1024)S(1)} %add.337, bf16[1024,4096]{1,0:T(8,128)(2,1)S(1)} %bitcast.106, f32[592,1024]{1,0:T(8,128)S(1)} %get-tuple-element.259, f32[1024]{0:T(1024)S(1)} %add.334, f32[1024]{0:T(1024)S(1)} %mul.440, f32[592]{0:T(1024)S(1)} %add_rsqrt_fusion, ...), kind=kOutput, calls=%fused_computation.9 | convolution fusion | flops 4983635968 | bytes 25391744 | tf_op jit(solution)/shard_map/icd,df->icf/dot_general | solution.py:306
  266.0 15.0 %copy.208 = bf16[16,256,2,512]{1,0,3,2:T(8,128)(2,1)} copy(bf16[16,256,2,512]{3,1,0,2:T(8,128)(2,1)} %get-tuple-element.226) | data formatting | bytes 16777216 | tf_op jit(solution)/shard_map/transpose | solution.py:269
  281.0 12.4 %copy.236 = bf16[128,8,16,256]{3,1,2,0:T(8,128)(2,1)} copy(bf16[128,8,16,256]{3,2,1,0:T(8,128)(2,1)} %bitcast.91) | data formatting | bytes 16777216
  293.4 12.3 %fusion.75 = (bf16[4096]{0:T(1024)(128)(2,1)S(1)}, bf16[592,4096]{1,0:T(8,128)(2,1)S(1)}) fusion(f32[592,4096]{1,0:T(8,128)} %get-tuple-element.261, f32[4096]{0:T(1024)S(1)} %add.337, bf16[4096,1024]{0,1:T(8,128)(2,1)} %bitcast.103, bf16[1,296,1,1,1,1,1024]{6,1,5,4,3,2,0:T(8,128)(2,1)} %bitcast.21, ...), kind=kOutput, calls=%fused_computation.160 | convolution fusion | flops 4998787072 | bytes 24176960 | tf_op jit(solution)/shard_map/icd,fd->icf/dot_general | solution.py:318
  305.7 9.7 %multiply_reduce_fusion.1 = (bf16[1024]{0:T(1024)(128)(2,1)S(1)}, f32[592]{0:T(1024)S(1)}, f32[592]{0:T(1024)S(1)}, bf16[1024]{0:T(1024)(128)(2,1)S(1)}, f32[592,1024]{1,0:T(8,128)}) fusion(f32[592,1024]{1,0:T(8,128)S(1)} %copy-done.8, f32[592]{0:T(1024)S(1)} %add_rsqrt_fusion, f32[592]{0:T(1024)S(1)} %broadcast_multiply_fusion.4, f32[1024]{0:T(1024)S(1)} %mul.440, ...), kind=kOutput, calls=%fused_computation.49 | convolution fusion | flops 4971508736 | bytes 18105600 | tf_op jit(solution)/shard_map/icf,df->icd/dot_general | solution.py:323
  315.4 9.6 %convolution_convert_fusion = bf16[1024,4096]{1,0:T(8,128)(2,1)} fusion(bf16[592,4096]{1,0:T(8,128)(2,1)S(1)} %get-tuple-element.265, f32[592,1024]{1,0:T(8,128)S(1)} %copy-done.8, f32[1024]{0:T(1024)S(1)} %add.334, f32[1024]{0:T(1024)S(1)} %mul.440, f32[592]{0:T(1024)S(1)} %add_rsqrt_fusion, f32[592]{0:T(1024)S(1)} %broadcast_multiply_fusion.4), kind=kOutput, calls=%fused_computation.13 | convolution fusion | flops 4973281280 | bytes 15676032 | tf_op jit(solution)/shard_map/icd,icf->df/dot_general | solution.py:322
  325.0 14.5 %reshape.707 = bf16[16,64,2,4,512]{4,3,2,1,0:T(4,128)(2,1)} reshape(bf16[1024,4096]{1,0:T(8,128)(2,1)} %convolution_convert_fusion) | data formatting | bytes 16777216 | tf_op jit(solution)/shard_map/reshape | solution.py:374
  339.5 13.0 %copy.240 = bf16[16,64,2,4,512]{4,2,1,3,0:T(2,128)(2,1)} copy(bf16[16,64,2,4,512]{4,3,2,1,0:T(4,128)(2,1)} %reshape.707) | data formatting | bytes 16777216 | tf_op jit(solution)/shard_map/reshape | solution.py:374
  352.6 14.3 %reshape.708 = bf16[16,256,1024]{2,1,0:T(8,128)(2,1)} reshape(bf16[16,4,64,2,512]{4,3,2,1,0:T(2,128)(2,1)} %bitcast.92) | data formatting | bytes 16777216 | tf_op jit(solution)/shard_map/reshape | solution.py:376
  366.8 9.1 %convolution_convert_fusion.1 = bf16[4096,1024]{1,0:T(8,128)(2,1)S(1)} fusion(bf16[592,4096]{1,0:T(8,128)(2,1)} %get-tuple-element.260, f32[592]{0:T(1024)S(1)} %fusion.52, bf16[296,1024]{1,0:T(8,128)(2,1)} %bitcast.19, bf16[296,1024]{1,0:T(8,128)(2,1)S(1)} %bitcast.117), kind=kOutput, calls=%fused_computation.14 | convolution fusion | flops 4973887488 | bytes 14453056 | tf_op jit(solution)/shard_map/icf,icd->fd/dot_general | solution.py:317
  381.3 16.6 %pad_maximum_fusion = bf16[16,576,1024]{2,1,0:T(8,128)(2,1)} fusion(bf16[16,256,1024]{2,1,0:T(8,128)(2,1)S(1)} %bitcast.108, bf16[16,256,1024]{2,1,0:T(8,128)(2,1)S(1)} %bitcast.94, bf16[16,64,1024]{2,1,0:T(8,128)(2,1)S(1)} %bitcast.119), kind=kLoop, calls=%fused_computation | loop fusion | flops 56623104 | bytes 37748736 | tf_op jit(solution)/shard_map/concatenate | solution.py:370
  405.6 33.4 %shard_map.396 = (f32[1,592,1024]{2,1,0:T(8,128)}, f32[1,592,1024]{2,1,0:T(8,128)}, f32[1,592,1024]{2,1,0:T(8,128)}) custom-call(bf16[1,592,1024]{2,1,0:T(8,128)(2,1)} %copy-done.2, bf16[1,592,1024]{2,1,0:T(8,128)(2,1)} %copy-done, bf16[1,592,1024]{2,1,0:T(8,128)(2,1)} %copy-done.1, bf16[1,592,1024]{2,1,0:T(8,128)(2,1)} %fusion.30.g_ref, ...), custom_call_target="tpu_custom_call" | custom-call | flops 7177502720 | bytes 12124160 | tf_op jit(solution)/shard_map/pallas_call | solution.py:135
  452.8 7.6 %convolution_convert_fusion.2 = bf16[1024,3072]{1,0:T(8,128)(2,1)S(1)} fusion(bf16[592,1024]{1,0:T(8,128)(2,1)} %copy-done.27, bf16[592,1024]{1,0:T(8,128)(2,1)} %copy-done.29, bf16[592,1024]{1,0:T(8,128)(2,1)} %copy-done.28, f32[1024]{0:T(1024)S(1)} %copy-done.58, f32[1024]{0:T(1024)S(1)} %copy-done.54, f32[592]{0:T(1024)S(1)} %copy-done.56, ...), kind=kOutput, calls=%fused_computation.17 | convolution fusion | flops 3744055296 | bytes 11154048 | tf_op jit(solution)/shard_map/icd,ice->de/dot_general | solution.py:344
  463.4 126.9 %reduce-scatter.5.cloned.1.call-done = bf16[576,1024]{1,0:T(8,128)(2,1)} async-done(((bf16[9216,1024]{1,0:T(8,128)(2,1)}), bf16[576,1024]{1,0:T(8,128)(2,1)}) %reduce-scatter.5.cloned.1.call-update) | async-done | bytes 1179664 | tf_op jit(solution)/shard_map/reduce_scatter | solution.py:381
  590.5 10.8 %fusion.31 = bf16[1,592,1024]{2,1,0:T(8,128)(2,1)S(1)} fusion(f32[592,1024]{1,0:T(8,128)} %copy-done.7, bf16[592,4096]{1,0:T(8,128)(2,1)} %get-tuple-element.260, bf16[4096,1024]{0,1:T(8,128)(2,1)} %bitcast.104, f32[1024]{0:T(1024)S(1)} %add.342), kind=kOutput, calls=%fused_computation.68 | convolution fusion | flops 4967874560 | bytes 16879616 | tf_op jit(solution)/shard_map/icf,fd->icd/dot_general | solution.py:312
  621.2 11.0 %collective-permute-done.3 = bf16[1,296,1024]{2,1,0:T(8,128)(2,1)S(1)} collective-permute-done((bf16[1,296,1024]{2,1,0:T(8,128)(2,1)}, bf16[1,296,1024]{2,1,0:T(8,128)(2,1)S(1)}, u32[]{:S(2)}, u32[]{:S(2)}) %collective-permute-start.3) | collective-permute-done | bytes 606240 | tf_op jit(solution)/shard_map/ppermute | solution.py:177
  633.0 10.6 %collective-permute-done.5 = bf16[576,512]{1,0:T(8,128)(2,1)} collective-permute-done((bf16[576,512]{1,0:T(8,128)(2,1)}, bf16[576,512]{1,0:T(8,128)(2,1)}, u32[]{:S(2)}, u32[]{:S(2)}) %collective-permute-start.5) | collective-permute-done | bytes 589856 | tf_op jit(solution)/shard_map/ppermute | solution.py:191
  648.9 31.1 %reduce-scatter.7.cloned.1.call-done = bf16[64,3200]{1,0:T(8,128)(2,1)} async-done(((bf16[1024,3200]{1,0:T(8,128)(2,1)}), bf16[64,3200]{1,0:T(8,128)(2,1)}) %reduce-scatter.7.cloned.1.call-update) | async-done | bytes 409616
  (254 shorter events, 126.1 us)
Async XLA Ops:
  7.2 77.9 %all-gather.3.cloned.1.call-start = ((), (), s32[]{:S(2)}) async-start(), calls=%async_computation.2 | async-start | bytes 7028736 | tf_op jit(solution)/shard_map/all_gather | solution.py:234
  9.8 75.4 %copy-start.30 = (bf16[2,296,1024]{2,1,0:T(8,128)(2,1)S(1)}, bf16[2,296,1024]{2,1,0:T(8,128)(2,1)}, u32[]{:S(2)}) copy-start(bf16[2,296,1024]{2,1,0:T(8,128)(2,1)} %param.20) | copy-start | bytes 3637252
  10.5 203.1 %all-gather.5.cloned.1.call-start = ((), (), s32[]{:S(2)}) async-start(), calls=%async_computation.3 | async-start | bytes 19464192 | tf_op jit(solution)/shard_map/all_gather | solution.py:247
  12.8 74.9 %copy-start.31 = (bf16[2,296,1024]{2,1,0:T(8,128)(2,1)S(1)}, bf16[2,296,1024]{2,1,0:T(8,128)(2,1)}, u32[]{:S(2)}) copy-start(bf16[2,296,1024]{2,1,0:T(8,128)(2,1)} %param.21) | copy-start | bytes 3637252
  85.2 505.2 %reduce-scatter.5.cloned.1.call-start = ((), (), s32[]{:S(2)}) async-start(), calls=%async_computation.4 | async-start | bytes 20054016 | tf_op jit(solution)/shard_map/reduce_scatter | solution.py:381
  86.2 21.0 %collective-permute-start = (bf16[1,296,1024]{2,1,0:T(8,128)(2,1)}, bf16[1,296,1024]{2,1,0:T(8,128)(2,1)S(1)}, u32[]{:S(2)}, u32[]{:S(2)}) collective-permute-start(bf16[1,296,1024]{2,1,0:T(8,128)(2,1)} %get-tuple-element.243), channel_id=1, source_target_pairs={{0,1},{1,0},{2,3},{3,2},{4,5},{5,4},{6,7},{7,6},{8,9},{9,8},{10,11... | collective-permute-start | bytes 1818632 | tf_op jit(solution)/shard_map/ppermute | solution.py:164
  88.8 204.6 %collective-permute-start.2 = (bf16[1,296,1024]{2,1,0:T(8,128)(2,1)}, bf16[1,296,1024]{2,1,0:T(8,128)(2,1)}, u32[]{:S(2)}, u32[]{:S(2)}) collective-permute-start(bf16[1,296,1024]{2,1,0:T(8,128)(2,1)} %get-tuple-element.239), channel_id=1, source_target_pairs={{0,1},{1,0},{2,3},{3,2},{4,5},{5,4},{6,7},{7,6},{8,9},{9,8},{10,11... | collective-permute-start | bytes 1818632 | tf_op jit(solution)/shard_map/ppermute | solution.py:164
  89.3 18.5 %copy-start.48 = (s32[296]{0:T(512)}, s32[296]{0:T(512)S(1)}, u32[]{:S(2)}) copy-start(s32[296]{0:T(512)S(1)} %iota_add_fusion) | copy-start | bytes 3556
  89.3 18.5 %copy-start.50 = (s32[296]{0:T(512)}, s32[296]{0:T(512)S(1)}, u32[]{:S(2)}) copy-start(s32[296]{0:T(512)S(1)} %iota_add_fusion.1) | copy-start | bytes 3556
  124.5 17.3 %copy-start.1 = (bf16[1,592,1024]{2,1,0:T(8,128)(2,1)}, bf16[1,592,1024]{2,1,0:T(8,128)(2,1)S(1)}, u32[]{:S(2)}) copy-start(bf16[1,592,1024]{2,1,0:T(8,128)(2,1)S(1)} %get-tuple-element.228.v_ref) | copy-start | bytes 3637252
  236.4 14.5 %copy-start.4 = (bf16[1,592,1024]{2,1,0:T(8,128)(2,1)S(1)}, bf16[1,592,1024]{2,1,0:T(8,128)(2,1)}, u32[]{:S(2)}) copy-start(bf16[1,592,1024]{2,1,0:T(8,128)(2,1)} %copy-done.3) | copy-start | bytes 3637252
  236.4 14.5 %copy-start.11 = (bf16[1,296,1024]{2,1,0:T(8,128)(2,1)S(1)}, bf16[1,296,1024]{2,1,0:T(8,128)(2,1)}, u32[]{:S(2)}) copy-start(bf16[1,296,1024]{2,1,0:T(8,128)(2,1)} %copy-done.10) | copy-start | bytes 1818628
  397.9 282.1 %reduce-scatter.7.cloned.1.call-start = ((), (), s32[]{:S(2)}) async-start(), calls=%async_computation.5 | async-start | bytes 6963200
  463.4 127.0 %copy-start.45 = (f32[1,16,2,32]{3,2,1,0:T(2,128)S(1)}, f32[1,16,2,32]{3,2,1,0:T(2,128)}, u32[]{:S(2)}) copy-start(f32[1,16,2,32]{3,2,1,0:T(2,128)} %get-tuple-element.248) | copy-start | bytes 12292
  602.4 16.9 %collective-permute-start.1 = (bf16[1,296,1024]{2,1,0:T(8,128)(2,1)}, bf16[1,296,1024]{2,1,0:T(8,128)(2,1)}, u32[]{:S(2)}, u32[]{:S(2)}) collective-permute-start(bf16[1,296,1024]{2,1,0:T(8,128)(2,1)} %get-tuple-element.240), channel_id=1, source_target_pairs={{0,1},{1,0},{2,3},{3,2},{4,5},{5,4},{6,7},{7,6},{8,9},{9,8},{10,11... | collective-permute-start | bytes 1818632 | tf_op jit(solution)/shard_map/ppermute | solution.py:177
  607.6 24.6 %collective-permute-start.3 = (bf16[1,296,1024]{2,1,0:T(8,128)(2,1)}, bf16[1,296,1024]{2,1,0:T(8,128)(2,1)S(1)}, u32[]{:S(2)}, u32[]{:S(2)}) collective-permute-start(bf16[1,296,1024]{2,1,0:T(8,128)(2,1)} %get-tuple-element.236), channel_id=1, source_target_pairs={{0,1},{1,0},{2,3},{3,2},{4,5},{5,4},{6,7},{7,6},{8,9},{9,8},{10,11... | collective-permute-start | bytes 1818632 | tf_op jit(solution)/shard_map/ppermute | solution.py:177
  610.0 33.6 %collective-permute-start.5 = (bf16[576,512]{1,0:T(8,128)(2,1)}, bf16[576,512]{1,0:T(8,128)(2,1)}, u32[]{:S(2)}, u32[]{:S(2)}) collective-permute-start(bf16[576,512]{1,0:T(8,128)(2,1)} %constant_dynamic-slice_fusion.2), channel_id=1, source_target_pairs={{0,1},{1,0},{2,3},{3,2},{4,5},{5,4},{6,7},{7,6},{8,9},{9,8},{10,11... | collective-permute-start | bytes 1769480 | tf_op jit(solution)/shard_map/ppermute | solution.py:191
  612.4 32.5 %copy-start.23 = (f32[256,512]{1,0:T(8,128)S(1)}, f32[256,512]{1,0:T(8,128)}, u32[]{:S(2)}) copy-start(f32[256,512]{1,0:T(8,128)} %param.25) | copy-start | bytes 1572868
  612.4 31.2 %copy-start.35 = (bf16[576,1024]{1,0:T(8,128)(2,1)S(1)}, bf16[576,1024]{1,0:T(8,128)(2,1)}, u32[]{:S(2)}) copy-start(bf16[576,1024]{1,0:T(8,128)(2,1)} %reduce-scatter.5.cloned.1.call-done) | copy-start | bytes 3538948
  612.4 32.4 %copy-start.36 = (f32[256,512]{1,0:T(8,128)S(1)}, f32[256,512]{1,0:T(8,128)}, u32[]{:S(2)}) copy-start(f32[256,512]{1,0:T(8,128)} %param.31) | copy-start | bytes 1572868
  612.5 32.4 %copy-start.37 = (f32[256,512]{1,0:T(8,128)S(1)}, f32[256,512]{1,0:T(8,128)}, u32[]{:S(2)}) copy-start(f32[256,512]{1,0:T(8,128)} %param.37) | copy-start | bytes 1572868
  647.5 39.0 %copy-start.52 = (f32[10,32]{1,0:T(8,128)S(1)}, f32[10,32]{1,0:T(8,128)}, u32[]{:S(2)}) copy-start(f32[10,32]{1,0:T(8,128)} %param.27) | copy-start | bytes 3844
  681.5 4.2 collective-permute-start.6
  684.3 9.9 %collective-permute-start.4 = (bf16[64,1536]{0,1:T(8,128)(2,1)S(1)}, bf16[64,1536]{0,1:T(8,128)(2,1)}, u32[]{:S(2)}, u32[]{:S(2)}) collective-permute-start(bf16[64,1536]{0,1:T(8,128)(2,1)S(1)} %copy.227), channel_id=1, source_target_pairs={{0,1},{1,0},{2,3},{3,2},{4,5},{5,4},{6,7},{7,6},{8,9},{9,8},{10,11... | collective-permute-start | bytes 589832 | tf_op jit(solution)/shard_map/ppermute | solution.py:191
  (50 other events, 219.8 us)
Sparse Core Ops, SparseCore 0:
  11.5 73.6 all-gather.2
  88.0 125.5 all-gather.4
  398.0 192.2 reduce-scatter.4
  594.1 85.8 reduce-scatter.6
